TPU v7x, 512 devices: a whole 4x4x16 slice. The times are simulated.
512 devices in a mesh: dp: 64 (over z, y), section: 2 (over core), mp: 4 (over x).
Axes of the slice: x: 4, y: 4, z: 16, core: 2. Of those that a mesh axis runs over, the one named last changes fastest.
Arguments:
- frames: bfloat16 [64, 128, 512], P('dp'), may hold values from -6 to 6
- lengths: int32 [64], P('dp'), may hold values from 32 to 128
- feature_proj: bfloat16 [512, 1920], P(None, 'mp'), may hold values from -0.25 to 0.25
- norm_gain: float32 [2, 1920], P('section'), may hold values from 0.25 to 1.75
- qkv_weight: bfloat16 [2, 1920, 5760], P('section', 'dp', 'mp'), may hold values from -0.125 to 0.125
- out_weight: bfloat16 [2, 1920, 1920], P('section', 'mp', 'dp'), may hold values from -0.125 to 0.125
- center: float32 [1920], replicated, may hold values from -4 to 4
- whitening: float32 [1920, 1024], P(None, 'dp'), may hold values from -0.125 to 0.125
Outputs:
- embeddings: float32 [64, 1024], P(None, 'dp')
All inputs are finite; a program needn't handle non-finite values.
Results may differ from a plain program's by a relative error of at most 0.0095.
Values may be sent and summed in bfloat16 or wider, within the bound.
No kernel may reach another device: no remote copies, remote signals or barrier semaphores. Data moves between devices by JAX's collectives and lax.ppermute only.
A program may use at most 64 MiB of HBM per device.

v0:
```python
import jax
import jax.numpy as jnp
from jax import lax
from jax.sharding import PartitionSpec as P

HD = 120


def passed_along(x, axis, by):
    count = lax.axis_size(axis)
    pairs = [(i, i + by) for i in range(count) if 0 <= i + by < count]
    return lax.ppermute(x, axis, pairs)


def broadcast(value, axis, source):
    kept = jnp.where(lax.axis_index(axis) == source, value, 0).astype(value.dtype)
    return lax.psum(kept, axis)


def layer_norm(values, gain):
    mean = jnp.mean(values, axis=-1, keepdims=True)
    centered = values - mean
    var = jnp.mean(centered * centered, axis=-1, keepdims=True)
    return centered * lax.rsqrt(var + 1e-05) * gain


def body(frames, lengths, feature_proj, norm_gain, qkv_weight, out_weight, center, whitening):
    section_index = lax.axis_index("section")
    gain = norm_gain[0]
    qkv_local = qkv_weight[0]
    out_local = out_weight[0]
    count_utt = frames.shape[0]
    frames_count = frames.shape[1]
    width = gain.shape[0]
    qkv_cols = qkv_local.shape[1]
    heads_local = qkv_cols // (3 * HD)
    full_qkv, full_out = (
        lax.all_gather(qkv_local, "dp", axis=0, tiled=True),
        lax.all_gather(out_local, "dp", axis=1, tiled=True),
    )
    received = jnp.zeros((frames_count, width), jnp.bfloat16)
    pooled_rows = []
    frame_ids = jnp.arange(frames_count, dtype=jnp.int32)
    for step in range(count_utt + 1):
        first_mb = min(step, count_utt - 1)
        second_mb = max(step - 1, 0)
        projected_part = jnp.dot(
            frames[first_mb], feature_proj, preferred_element_type=jnp.float32
        ).astype(jnp.bfloat16)
        projected = lax.all_gather(projected_part, "mp", axis=1, tiled=True)
        first_section = section_index == 0
        layer_input = jnp.where(first_section, projected, received)
        length = jnp.where(first_section, lengths[first_mb], lengths[second_mb])
        normed = layer_norm(layer_input.astype(jnp.float32), gain).astype(jnp.bfloat16)
        qkv_sum = jnp.dot(normed, full_qkv, preferred_element_type=jnp.float32)
        qkv = qkv_sum.astype(jnp.bfloat16).reshape(frames_count, 3, heads_local, HD)
        query = qkv[:, 0]
        keys = qkv[:, 1]
        values = qkv[:, 2]
        scores = jnp.einsum(
            "qhd,khd->hqk", query, keys, preferred_element_type=jnp.float32
        ) / jnp.sqrt(jnp.float32(HD))
        attention_valid = jnp.arange(frames_count, dtype=jnp.int32) < length
        scores = jnp.where(attention_valid[None, None, :], scores, jnp.float32(-1e30))
        probs = jax.nn.softmax(scores, axis=-1).astype(jnp.bfloat16)
        context = jnp.einsum(
            "hqk,khd->qhd", probs, values, preferred_element_type=jnp.float32
        ).astype(jnp.bfloat16)
        context = context.reshape(frames_count, heads_local * HD)
        partial_out = jnp.dot(context, full_out, preferred_element_type=jnp.float32)
        attended = lax.psum(partial_out.astype(jnp.bfloat16), "mp").astype(jnp.float32)
        result = (layer_input.astype(jnp.float32) + attended).astype(jnp.bfloat16)
        if step >= 1:
            valid = frame_ids < lengths[step - 1]
            summed = jnp.sum(
                jnp.where(valid[:, None], result.astype(jnp.float32), jnp.float32(0.0)), axis=0
            )
            pooled_rows.append(summed / lengths[step - 1].astype(jnp.float32))
        if step < count_utt:
            received = passed_along(result, "section", 1)
    pooled = jnp.stack(pooled_rows, axis=0)
    pooled = broadcast(pooled, "section", 1)
    return jnp.dot(
        lax.all_gather(pooled, "dp", axis=0, tiled=True) - center,
        whitening,
        precision=lax.Precision.HIGHEST,
        preferred_element_type=jnp.float32,
    )


def solution(mesh):
    in_specs = (
        P("dp", None, None),
        P("dp"),
        P(None, "mp"),
        P("section", None),
        P("section", "dp", "mp"),
        P("section", "mp", "dp"),
        P(),
        P(None, "dp"),
    )
    out_specs = P(None, "dp")
    return jax.shard_map(body, mesh=mesh, in_specs=in_specs, out_specs=out_specs, check_vma=False)
```

profile of v0, /device:TPU:4, one launch (start us, length us, event | category | flops | bytes accessed | tf_op | source)
XLA Modules:
  0.0 596.0 jit_solution(13150222934486986474)
XLA Ops:
  6.5 1.5 copy.22
  8.1 1.7 copy.19
  11.3 1.2 convolution_convert_fusion.2
  12.5 16.5 %all_gather.13 = bf16[128,1920]{0,1:T(8,128)(2,1)S(1)} all-gather(bf16[128,480]{0,1:T(8,128)(2,1)S(1)} %convolution_convert_fusion.2), channel_id=1, replica_groups=mesh['dp'=64,'section'=2,'mp'=4] {'mp'}, dimensions={1}, use_global_device_ids=true | all-gather | bytes 614400 | tf_op jit(solution)/shard_map/all_gather | solution.py:50
  29.6 131.5 %all-gather.8.cloned.1.call-done = bf16[1,480,1920]{1,0,2:T(2,128)(2,1)} async-done(((bf16[1,480,30]{1,0,2:T(2,128)(2,1)}), bf16[1,480,1920]{1,0,2:T(2,128)(2,1)}) %all-gather.8.cloned.1.call-update) | async-done | bytes 1843216 | tf_op jit(solution)/shard_map/all_gather | solution.py:39
  161.1 7.6 %copy.23 = bf16[1,480,1920]{2,1,0:T(8,128)(2,1)S(1)} copy(bf16[1,480,1920]{1,0,2:T(2,128)(2,1)} %all-gather.8.cloned.1.call-done) | data formatting | bytes 3686400 | tf_op jit(solution)/shard_map/all_gather | solution.py:39
  168.7 157.5 %all-gather.6.cloned.1.call-done = bf16[1,1920,1440]{2,0,1:T(2,128)(2,1)} async-done(((bf16[1,30,1440]{2,0,1:T(2,128)(2,1)}), bf16[1,1920,1440]{2,0,1:T(2,128)(2,1)}) %all-gather.6.cloned.1.call-update) | async-done | bytes 5529616 | tf_op jit(solution)/shard_map/all_gather | solution.py:38
  326.2 23.4 %copy.20 = bf16[1,1920,1440]{1,2,0:T(8,128)(2,1)} copy(bf16[1,1920,1440]{2,0,1:T(2,128)(2,1)} %all-gather.6.cloned.1.call-done) | data formatting | bytes 11059200 | tf_op jit(solution)/shard_map/all_gather | solution.py:38
  349.6 4.3 fusion.9
  354.4 0.9 convolution_convert_fusion.4
  355.3 2.6 convolution_convert_fusion.1
  357.9 52.0 %all-reduce.3.cloned.1.call-done = bf16[128,1920]{0,1:T(8,128)(2,1)} async-done(((bf16[128,1920]{0,1:T(8,128)(2,1)}), bf16[128,1920]{0,1:T(8,128)(2,1)}) %all-reduce.3.cloned.1.call-update) | async-done | bytes 491536 | tf_op jit(solution)/shard_map/psum | solution.py:71
  410.0 1.2 fusion.30
  411.2 1.3 collective-permute-start
  412.5 1.4 collective-permute-done
  414.5 4.3 fusion.6
  419.9 1.2 fusion.16
  421.1 1.1 convolution_convert_fusion.3
  422.2 1.7 convolution_convert_fusion
  423.9 59.0 %all-reduce.5.cloned.1.call-done = bf16[128,1920]{0,1:T(8,128)(2,1)} async-done(((bf16[128,1920]{0,1:T(8,128)(2,1)}), bf16[128,1920]{0,1:T(8,128)(2,1)}) %all-reduce.5.cloned.1.call-update) | async-done | bytes 491536 | tf_op jit(solution)/shard_map/psum | solution.py:71
  483.0 1.4 select_reduce_fusion
  484.4 2.5 psum.23
  486.9 101.4 %all-gather.2 = f32[64,1,1920]{2,1,0:T(1,128)S(1)} all-gather(f32[1,1,1920]{2,1,0:T(1,128)S(1)} %bitcast.80), channel_id=1, replica_groups=mesh['dp'=64,'section'=2,'mp'=4] {'dp'}, dimensions={0}, use_global_device_ids=true | all-gather | bytes 499200 | tf_op jit(solution)/shard_map/all_gather | solution.py:84
  588.3 1.1 fusion.34
  (31 shorter events, 3.6 us)
Async XLA Ops:
  6.5 4.7 copy-start
  6.5 154.6 %all-gather.8.cloned.1.call-start = ((), (), s32[]{:S(2)}) async-start(), calls=%async_computation.3 | async-start | bytes 3993600 | tf_op jit(solution)/shard_map/all_gather | solution.py:39
  8.0 318.1 %all-gather.6.cloned.1.call-start = ((), (), s32[]{:S(2)}) async-start(), calls=%async_computation.2 | async-start | bytes 11980800 | tf_op jit(solution)/shard_map/all_gather | solution.py:38
  9.8 400.1 %all-reduce.3.cloned.1.call-start = ((), (), s32[]{:S(2)}) async-start(), calls=%async_computation | async-start | bytes 983040 | tf_op jit(solution)/shard_map/psum | solution.py:71
  357.9 125.1 %all-reduce.5.cloned.1.call-start = ((), (), s32[]{:S(2)}) async-start(), calls=%async_computation.1 | async-start | bytes 983040 | tf_op jit(solution)/shard_map/psum | solution.py:71
  411.2 2.8 collective-permute-start
  414.5 173.8 %copy-start.2 = (f32[1920,16]{0,1:T(8,128)S(1)}, f32[1920,16]{0,1:T(8,128)}, u32[]{:S(2)}) copy-start(f32[1920,16]{0,1:T(8,128)} %param.15) | copy-start | bytes 368644
  414.5 173.8 %copy-start.3 = (f32[1920]{0:T(1024)S(1)}, f32[1920]{0:T(1024)}, u32[]{:S(2)}) copy-start(f32[1920]{0:T(1024)} %param.14) | copy-start | bytes 23044
  418.8 0.7 copy-start.1
Sparse Core Ops, SparseCore 0:
  10.3 150.7 all-gather.7
  164.1 162.0 all-gather.5
  358.0 51.9 all-reduce.2
  424.1 58.8 all-reduce.4
where the time goes:
time: 597 us; the launch traced here: 596 us
  waiting for transfers between devices  402 us (67%)
  blocking collectives  120 us (20%)
  local copies, waits for them, and re-layouts  34.9 us (6%)
  matrix products  19.3 us (3%)
  between operations  13.9 us (2%)
    all_gather x1, waiting for transfers between devices, body(): lax.all_gather(qkv_local, 'dp', axis=0, tiled=True)  157 us
    all_gather x1, waiting for transfers between devices, body(): lax.all_gather(out_local, 'dp', axis=1, tiled=True)  132 us
    psum x2, waiting for transfers between devices, body(): lax.psum(partial_out.astype(jnp.bfloat16), 'mp').astype(jnp.float32)  111 us
    all_gather x1, blocking collectives, body(): lax.all_gather(pooled, 'dp', axis=0, tiled=True) - center  101 us
    all_gather x1, local copies, waits for them, and re-layouts, body(): lax.all_gather(qkv_local, 'dp', axis=0, tiled=True)  23.4 us
    all_gather x1, blocking collectives, body(): projected = lax.all_gather(projected_part, 'mp', axis=1, tiled=True)  16.5 us
  transfers between devices with their start and end apart: 5, of which 5 were waited for; matrix products, arithmetic and copies ran while one was open for 2% of the time, Pallas kernels for 0%

commit v1 on v0

--- a/solution.py
+++ b/solution.py
@@ -1,9 +1,17 @@
+import functools
 import jax
 import jax.numpy as jnp
 from jax import lax
 from jax.sharding import PartitionSpec as P
 
 HD = 120
+
+
+def name_the_ranges(view, mesh_ax):
+    return jnp.sum(lax.all_gather(view, mesh_ax), axis=0)
+
+
+_place_set = functools.partial(name_the_ranges, mesh_ax="mp")
 
 
 def passed_along(x, axis, by):
@@ -68,7 +76,7 @@
         ).astype(jnp.bfloat16)
         context = context.reshape(frames_count, heads_local * HD)
         partial_out = jnp.dot(context, full_out, preferred_element_type=jnp.float32)
-        attended = lax.psum(partial_out.astype(jnp.bfloat16), "mp").astype(jnp.float32)
+        attended = _place_set(partial_out.astype(jnp.bfloat16)).astype(jnp.float32)
         result = (layer_input.astype(jnp.float32) + attended).astype(jnp.bfloat16)
         if step >= 1:
             valid = frame_ids < lengths[step - 1]

time: 597 us -> 559 us (0.936)
  the two profiles are of different devices: /device:TPU:4 before, /device:TPU:8 now
where the time goes in v1:
time: 559 us; the launch traced here: 557 us
  waiting for transfers between devices  364 us (65%)
  blocking collectives  116 us (21%)
  local copies, waits for them, and re-layouts  36.2 us (6%)
  matrix products  18.4 us (3%)
  between operations  13.9 us (2%)
  other arithmetic  7.14 us (1%)
    all_gather x1, waiting for transfers between devices, body(): lax.all_gather(qkv_local, 'dp', axis=0, tiled=True)  157 us
    all_gather x1, waiting for transfers between devices, body(): lax.all_gather(out_local, 'dp', axis=1, tiled=True)  134 us
    all_gather x1, blocking collectives, body(): lax.all_gather(pooled, 'dp', axis=0, tiled=True) - center  101 us
    all_gather x2, waiting for transfers between devices, name_the_ranges(): return jnp.sum(lax.all_gather(view, mesh_ax), axis=0)  70.9 us
    all_gather x1, local copies, waits for them, and re-layouts, body(): lax.all_gather(qkv_local, 'dp', axis=0, tiled=True)  23.4 us
    all_gather x1, blocking collectives, body(): projected = lax.all_gather(projected_part, 'mp', axis=1, tiled=True)  13.1 us
  transfers between devices with their start and end apart: 5, of which 5 were waited for; matrix products, arithmetic and copies ran while one was open for 2% of the time, Pallas kernels for 0%

profile of v1, /device:TPU:8, one launch (start us, length us, event | category | flops | bytes accessed | tf_op | source)
XLA Modules:
  0.0 557.3 jit_solution(16892474857828097255)
XLA Ops:
  6.5 1.5 copy.20
  8.1 1.7 copy.17
  11.3 1.2 convolution_convert_fusion.2
  12.5 13.1 %all_gather.25 = bf16[128,1920]{0,1:T(8,128)(2,1)S(1)} all-gather(bf16[128,480]{0,1:T(8,128)(2,1)S(1)} %convolution_convert_fusion.2), channel_id=1, replica_groups=mesh['dp'=64,'section'=2,'mp'=4] {'mp'}, dimensions={1}, use_global_device_ids=true | all-gather | bytes 614400 | tf_op jit(solution)/shard_map/all_gather | solution.py:58
  26.1 133.6 %all-gather.12.cloned.1.call-done = bf16[1,480,1920]{1,0,2:T(2,128)(2,1)} async-done(((bf16[1,480,30]{1,0,2:T(2,128)(2,1)}), bf16[1,480,1920]{1,0,2:T(2,128)(2,1)}) %all-gather.12.cloned.1.call-update) | async-done | bytes 1843216 | tf_op jit(solution)/shard_map/all_gather | solution.py:47
  159.7 7.6 %copy.21 = bf16[1,480,1920]{2,1,0:T(8,128)(2,1)S(1)} copy(bf16[1,480,1920]{1,0,2:T(2,128)(2,1)} %all-gather.12.cloned.1.call-done) | data formatting | bytes 3686400 | tf_op jit(solution)/shard_map/all_gather | solution.py:47
  167.3 157.5 %all-gather.10.cloned.1.call-done = bf16[1,1920,1440]{2,0,1:T(2,128)(2,1)} async-done(((bf16[1,30,1440]{2,0,1:T(2,128)(2,1)}), bf16[1,1920,1440]{2,0,1:T(2,128)(2,1)}) %all-gather.10.cloned.1.call-update) | async-done | bytes 5529616 | tf_op jit(solution)/shard_map/all_gather | solution.py:46
  324.8 23.4 %copy.18 = bf16[1,1920,1440]{1,2,0:T(8,128)(2,1)} copy(bf16[1,1920,1440]{2,0,1:T(2,128)(2,1)} %all-gather.10.cloned.1.call-done) | data formatting | bytes 11059200 | tf_op jit(solution)/shard_map/all_gather | solution.py:46
  348.2 4.3 fusion.9
  353.9 2.2 convolution_convert_fusion.1
  356.2 33.2 %all-gather.14.cloned.1.call-done = bf16[512,1920]{1,0:T(8,128)(2,1)} async-done(((bf16[128,1920]{1,0:T(8,128)(2,1)}), bf16[512,1920]{1,0:T(8,128)(2,1)}) %all-gather.14.cloned.1.call-update) | async-done | bytes 1966096 | tf_op jit(solution)/shard_map/all_gather | solution.py:11
  389.4 1.9 reduce_sum.90
  392.3 1.2 fusion.30
  393.5 1.8 collective-permute-start
  395.2 1.4 collective-permute-done
  397.3 4.3 fusion.6
  402.6 1.2 fusion.16
  403.8 1.1 convolution_convert_fusion.3
  405.0 1.3 convolution_convert_fusion
  406.3 37.7 %all-gather.16.cloned.1.call-done = bf16[512,1920]{1,0:T(8,128)(2,1)} async-done(((bf16[128,1920]{1,0:T(8,128)(2,1)}), bf16[512,1920]{1,0:T(8,128)(2,1)}) %all-gather.16.cloned.1.call-update) | async-done | bytes 1966096 | tf_op jit(solution)/shard_map/all_gather | solution.py:11
  443.9 1.9 reduce_sum.94
  446.5 2.5 psum.7
  449.0 100.6 %all-gather.4 = f32[64,1,1920]{2,1,0:T(1,128)S(1)} all-gather(f32[1,1,1920]{2,1,0:T(1,128)S(1)} %bitcast.84), channel_id=1, replica_groups=mesh['dp'=64,'section'=2,'mp'=4] {'dp'}, dimensions={0}, use_global_device_ids=true | all-gather | bytes 499200 | tf_op jit(solution)/shard_map/all_gather | solution.py:92
  549.6 1.1 fusion.34
  (35 shorter events, 6.1 us)
Async XLA Ops:
  6.5 4.7 copy-start
  6.5 153.2 %all-gather.12.cloned.1.call-start = ((), (), s32[]{:S(2)}) async-start(), calls=%async_computation.1 | async-start | bytes 3993600 | tf_op jit(solution)/shard_map/all_gather | solution.py:47
  8.0 316.8 %all-gather.10.cloned.1.call-start = ((), (), s32[]{:S(2)}) async-start(), calls=%async_computation | async-start | bytes 11980800 | tf_op jit(solution)/shard_map/all_gather | solution.py:46
  9.8 379.6 %all-gather.14.cloned.1.call-start = ((), (), s32[]{:S(2)}) async-start(), calls=%async_computation.2 | async-start | bytes 2457600 | tf_op jit(solution)/shard_map/all_gather | solution.py:11
  356.1 87.8 %all-gather.16.cloned.1.call-start = ((), (), s32[]{:S(2)}) async-start(), calls=%async_computation.3 | async-start | bytes 2457600 | tf_op jit(solution)/shard_map/all_gather | solution.py:11
  393.5 3.2 collective-permute-start
  401.5 0.7 copy-start.1
  404.9 144.7 %copy-start.2 = (f32[1920,16]{0,1:T(8,128)S(1)}, f32[1920,16]{0,1:T(8,128)}, u32[]{:S(2)}) copy-start(f32[1920,16]{0,1:T(8,128)} %param.15) | copy-start | bytes 368644
  404.9 144.7 %copy-start.3 = (f32[1920]{0:T(1024)S(1)}, f32[1920]{0:T(1024)}, u32[]{:S(2)}) copy-start(f32[1920]{0:T(1024)} %param.14) | copy-start | bytes 23044
Sparse Core Ops, SparseCore 0:
  10.3 149.3 all-gather.11
  162.7 162.1 all-gather.9
  356.3 33.1 all-gather.13
  406.4 37.5 all-gather.15
